TPU v7x, 256 devices: a whole 4x4x8 slice. The times are simulated.
256 devices in a mesh: win: 32 (over y, x, core), grp: 8 (over z).
Axes of the slice: x: 4, y: 4, z: 8, core: 2. Of those that a mesh axis runs over, the one named last changes fastest.
Arguments:
- traces: bfloat16 [256, 512, 2048], P(('win', 'grp'))
- pair_lists: int32 [32, 3], P('win'), may hold values from -1 to 3, as said below
- observed: float32 [32, 3, 16, 16, 2048], P('win'), may hold values from -4 to 4
Outputs:
- correl: float32 [32, 3, 16, 16, 2048], P('win', None, None, None, 'grp')
- trace_gradient: bfloat16 [256, 512, 2048], P(('win', 'grp'))
Inputs may be any that keep to these rules, and one draw needn't show every extreme that they name: `pair_lists`: each row lists distinct offsets in increasing order, followed by -1 in its empty slots; block a lists only offsets o with a + o < 32; every block lists at least one offset, and block 0 fills all 3 slots and lists offset 4 - 1.
All inputs are finite; a program needn't handle non-finite values.
Results may differ from a plain program's by a relative error of at most 0.014.
Values may be sent and summed in bfloat16 or wider, within the bound.
No kernel may reach another device: no remote copies, remote signals or barrier semaphores. Data moves between devices by JAX's collectives and lax.ppermute only.
A program may use at most 192 MiB of HBM per device.

v0:
```python
import math
import jax
import jax.numpy as jnp
from jax import lax
from jax.sharding import PartitionSpec as P

SEG = 2048
FREQ = 1024
BAND = 64
OFFSETS = 4


def passed_along(array, axis, by):
    peers = lax.axis_size(axis)
    pairs = [(i, i + by) for i in range(peers) if 0 <= i + by < peers]
    return lax.ppermute(array, axis, pairs)


def dft_table(first_column, column_count):
    samples = jnp.arange(SEG, dtype=jnp.int32)
    columns = first_column + jnp.arange(column_count, dtype=jnp.int32)
    harmonic = columns % FREQ
    phases = samples[:, None] * harmonic[None, :] % SEG
    angles = phases.astype(jnp.float32) * (2.0 * math.pi / SEG)
    values = jnp.where(columns[None, :] < FREQ, jnp.cos(angles), -jnp.sin(angles))
    return values.astype(jnp.bfloat16)


def whiten(spectrum):
    halfway = spectrum.shape[-1] // 2
    real_part = spectrum[..., :halfway]
    imag_part = spectrum[..., halfway:]
    power_bins = real_part * real_part + imag_part * imag_part
    banded = power_bins.reshape(power_bins.shape[:-1] + (halfway // BAND, BAND))
    inverse = lax.rsqrt(jnp.mean(banded, axis=-1) + 1e-05)
    spread = jnp.broadcast_to(inverse[..., None], banded.shape).reshape(power_bins.shape)
    return spectrum * jnp.concatenate([spread, spread], axis=-1)


def split_halves(operand):
    halfway = operand.shape[-1] // 2
    return (operand[..., :halfway], operand[..., halfway:])


def widen(operand):
    return operand.astype(jnp.float32)


def correlate(leading, trailing, windows_total):
    lead_real, lead_imag = split_halves(leading)
    trail_real, trail_imag = split_halves(trailing)
    left_real = widen(lead_real)[:, :, None, :]
    left_imag = widen(lead_imag)[:, :, None, :]
    right_real = widen(trail_real)[:, None, :, :]
    right_imag = widen(trail_imag)[:, None, :, :]
    real_sum = jnp.sum(left_real * right_real + left_imag * right_imag, axis=0)
    imag_sum = jnp.sum(left_real * right_imag - left_imag * right_real, axis=0)
    return jnp.concatenate([real_sum, imag_sum], axis=-1) / windows_total


def pull_first(residual, trailing):
    resid_real, resid_imag = split_halves(residual)
    trail_real, trail_imag = split_halves(trailing)
    left_real = widen(resid_real)[None]
    left_imag = widen(resid_imag)[None]
    right_real = widen(trail_real)[:, None, :, :]
    right_imag = widen(trail_imag)[:, None, :, :]
    real_part = jnp.sum(left_real * right_real + left_imag * right_imag, axis=2)
    imag_part = jnp.sum(left_real * right_imag - left_imag * right_real, axis=2)
    return jnp.concatenate([real_part, imag_part], axis=-1)


def pull_second(residual, leading):
    resid_real, resid_imag = split_halves(residual)
    lead_real, lead_imag = split_halves(leading)
    left_real = widen(resid_real)[None]
    left_imag = widen(resid_imag)[None]
    right_real = widen(lead_real)[:, :, None, :]
    right_imag = widen(lead_imag)[:, :, None, :]
    real_part = jnp.sum(left_real * right_real - left_imag * right_imag, axis=1)
    imag_part = jnp.sum(left_real * right_imag + left_imag * right_real, axis=1)
    return jnp.concatenate([real_part, imag_part], axis=-1)


def on_device(traces, pair_lists, observed):
    win_dev, channels, samples = traces.shape
    column_total = 2 * FREQ
    column_step = min(512, column_total)
    tables = [
        dft_table(start_col, column_step) for start_col in range(0, column_total, column_step)
    ]
    flat_traces = traces.reshape(win_dev * channels, samples)
    spectra = jnp.concatenate(
        [
            jnp.dot(flat_traces, table_part, preferred_element_type=jnp.float32)
            for table_part in tables
        ],
        axis=1,
    )
    spectra = spectra.reshape(win_dev, channels, column_total)
    whitened = whiten(spectra).astype(jnp.bfloat16)
    grp_count = lax.axis_size("grp")
    share_width = column_total // grp_count
    moved_blocks = lax.all_to_all(whitened, "win", split_axis=1, concat_axis=0, tiled=True)
    windows_total = moved_blocks.shape[0] * grp_count
    partner_list = [moved_blocks] + [
        passed_along(moved_blocks, "win", -offset) for offset in range(1, OFFSETS)
    ]
    stacked = jnp.stack(partner_list)
    offsets = pair_lists[0]
    slot_total = offsets.shape[0]
    live_slots = (offsets >= 0).astype(jnp.float32)[:, None, None, None]
    partners = [
        lax.dynamic_index_in_dim(stacked, jnp.maximum(offsets[slot_index], 0), 0, keepdims=False)
        for slot_index in range(slot_total)
    ]
    correl = (
        jnp.stack(
            [correlate(moved_blocks, partner_block, windows_total) for partner_block in partners]
        )
        * live_slots
    )
    share_start = lax.axis_index("grp") * share_width
    totals = lax.psum(correl, "grp")
    correl_share = lax.dynamic_slice_in_dim(totals, share_start, share_width, 3)
    residual = ((totals - observed[0]) * live_slots).astype(jnp.bfloat16)
    own_grad = pull_first(residual[0], partners[0])
    for slot_index in range(1, slot_total):
        own_grad = own_grad + pull_first(residual[slot_index], partners[slot_index])
    contrib = []
    for offset in range(OFFSETS):
        chosen = jnp.zeros_like(residual[0])
        for slot_index in range(slot_total):
            chosen = jnp.where(offsets[slot_index] == offset, residual[slot_index], chosen)
        contrib.append(pull_second(chosen, moved_blocks))
    white_grad = own_grad + contrib[0]
    for offset in range(1, OFFSETS):
        white_grad = white_grad + passed_along(
            contrib[offset].astype(jnp.bfloat16), "win", offset
        ).astype(jnp.float32)
    returned = lax.all_to_all(
        white_grad.astype(jnp.bfloat16), "win", split_axis=0, concat_axis=1, tiled=True
    )
    unused, pullback = jax.vjp(whiten, spectra)
    spectra_grad = pullback(returned.astype(jnp.float32))[0].astype(jnp.bfloat16)
    flat_grad = spectra_grad.reshape(win_dev * channels, column_total)
    trace_grad = jnp.zeros((win_dev * channels, samples), jnp.float32)
    for table_index in range(len(tables)):
        start_col = table_index * column_step
        trace_grad = trace_grad + jnp.dot(
            flat_grad[:, start_col : start_col + column_step],
            tables[table_index].T,
            preferred_element_type=jnp.float32,
        )
    return (correl_share[None], trace_grad.reshape(win_dev, channels, samples).astype(jnp.bfloat16))


def solution(mesh):
    return jax.shard_map(
        on_device,
        mesh=mesh,
        in_specs=(P(("win", "grp"), None, None), P("win", None), P("win", None, None, None, None)),
        out_specs=(P("win", None, None, None, "grp"), P(("win", "grp"), None, None)),
        check_vma=False,
    )
```

profile of v0, /device:TPU:1, one launch (start us, length us, event | category | flops | bytes accessed | tf_op | source)
XLA Modules:
  0.0 817.0 jit_solution(5095351248463171921)
XLA Ops:
  7.3 1.4 copy-done
  8.8 17.5 %fusion.41 = f32[512,512]{1,0:T(8,128)S(1)} fusion(bf16[1,512,2048]{2,1,0:T(8,128)(2,1)S(1)} %copy-done, s32[512]{0:T(512)S(1)} %add_select_fusion.4, pred[512]{0:T(512)(128)(4,1)S(1)} %fusion.60), kind=kOutput, calls=%fused_computation.95 | convolution fusion | flops 1091567616 | bytes 3148288 | tf_op jit(solution)/shard_map/dot_general | solution.py:95
  26.2 17.2 %fusion.43 = f32[512,512]{1,0:T(8,128)S(1)} fusion(bf16[1,512,2048]{2,1,0:T(8,128)(2,1)S(1)} %copy-done, s32[512]{0:T(512)S(1)} %add_select_fusion.5, pred[512]{0:T(512)(128)(4,1)S(1)} %fusion.61), kind=kOutput, calls=%fused_computation.97 | convolution fusion | flops 1091567616 | bytes 3148288 | tf_op jit(solution)/shard_map/dot_general | solution.py:95
  43.4 17.6 %fusion.45 = f32[512,512]{1,0:T(8,128)S(1)} fusion(bf16[1,512,2048]{2,1,0:T(8,128)(2,1)S(1)} %copy-done, s32[512]{0:T(512)S(1)} %add_select_fusion.6, pred[512]{0:T(512)(128)(4,1)S(1)} %fusion.62), kind=kOutput, calls=%fused_computation.99 | convolution fusion | flops 1091567616 | bytes 3148288 | tf_op jit(solution)/shard_map/dot_general | solution.py:95
  61.0 17.2 %fusion.47 = f32[512,512]{1,0:T(8,128)S(1)} fusion(bf16[1,512,2048]{2,1,0:T(8,128)(2,1)S(1)} %copy-done, s32[512]{0:T(512)S(1)} %add_select_fusion.7, pred[512]{0:T(512)(128)(4,1)S(1)} %iota_compare_fusion), kind=kOutput, calls=%fused_computation.101 | convolution fusion | flops 1091567616 | bytes 3148288 | tf_op jit(solution)/shard_map/dot_general | solution.py:95
  78.7 0.5 copy-done.17
  79.2 2.0 copy-done.3
  81.2 0.9 multiply_add_fusion
  82.7 3.9 fusion.16
  86.6 10.8 %copy.14 = bf16[1,512,2048]{2,0,1:T(2,128)(2,1)} copy(bf16[1,512,2048]{1,2,0:T(8,128)(2,1)} %fusion.16) | data formatting | bytes 4194304 | tf_op jit(solution)/shard_map/convert_element_type | solution.py:101
  97.4 0.5 broadcast.306
  98.0 13.2 %reduce.2 = bf16[512,2048]{1,0:T(8,128)(2,1)S(1)} reduce(bf16[512,1,2048]{2,1,0:T(2,128)(2,1)} %bitcast.118, bf16[]{:T(256)} %broadcast.306), dimensions={1}, to_apply=%bitcast.108.reduce_sub_computation | reduce | bytes 4194306
  111.1 2.8 reshape.499
  113.9 37.0 %all_to_all.21 = bf16[32,2,16384]{2,1,0:T(2,128)(2,1)S(1)} all-to-all(bf16[32,2,16384]{2,1,0:T(2,128)(2,1)} %reshape.499), channel_id=1, replica_groups=mesh['win'=32,'grp'=8] {'win'}, dimensions={0} | all-to-all | bytes 4194304 | tf_op jit(solution)/shard_map/all_to_all | solution.py:104
  150.9 6.8 reshape.500
  157.6 3.5 copy.17
  161.1 1.3 collective-permute-start.2
  162.4 1.3 collective-permute-start.1
  163.7 2.3 collective-permute-start
  166.0 0.6 fusion.99
  168.5 2.5 slice_convert_fusion.7
  171.1 18.9 %collective-permute-done.2 = bf16[32,16,2048]{2,1,0:T(8,128)(2,1)S(1)} collective-permute-done((bf16[32,16,2048]{2,1,0:T(8,128)(2,1)S(1)}, bf16[32,16,2048]{2,1,0:T(8,128)(2,1)S(1)}, u32[]{:S(2)}, u32[]{:S(2)}) %collective-permute-start.2) | collective-permute-done | bytes 2097184 | tf_op jit(solution)/shard_map/ppermute | solution.py:16
  190.0 63.7 %collective-permute-done.1 = bf16[32,16,2048]{2,1,0:T(8,128)(2,1)S(1)} collective-permute-done((bf16[32,16,2048]{2,1,0:T(8,128)(2,1)S(1)}, bf16[32,16,2048]{2,1,0:T(8,128)(2,1)S(1)}, u32[]{:S(2)}, u32[]{:S(2)}) %collective-permute-start.1) | collective-permute-done | bytes 2097184 | tf_op jit(solution)/shard_map/ppermute | solution.py:16
  253.7 1.9 collective-permute-done
  255.6 1.1 pad_maximum_fusion
  256.7 1.1 dynamic-slice_bitcast_fusion
  257.8 1.8 slice_convert_fusion.6
  259.6 3.7 slice_convert_fusion
  263.3 35.8 %add_reduce_fusion.9 = (f32[16,16,1024]{2,1,0:T(8,128)}, f32[16,16,1024]{2,1,0:T(8,128)}, f32[16,16,1024]{2,1,0:T(8,128)}, f32[16,16,1024]{2,1,0:T(8,128)}, f32[16,16,1024]{2,1,0:T(8,128)}, /*index=5*/f32[16,16,1024]{2,1,0:T(8,128)}) fusion(f32[32,16,1024]{2,1,0:T(8,128)} %get-tuple-element.50, f32[32,16,1024]{2,1,0:T(8,128)} %get-tuple-element.48, ...), kind=kLoop, calls=%fused_computation.19 | loop fusion | flops 199753728 | bytes 23068672 | tf_op jit(solution)/shard_map/reduce_sum | solution.py:56
  299.1 1.8 maximum_multiply_fusion.1
  302.1 3.4 maximum_multiply_fusion
  313.0 164.2 %all-reduce.4.cloned.1.call-done = f32[3,16,16,2048]{3,2,1,0:T(8,128)} async-done(((f32[3,16,16,2048]{3,2,1,0:T(8,128)}), f32[3,16,16,2048]{3,2,1,0:T(8,128)}) %all-reduce.4.cloned.1.call-update) | async-done | bytes 6291472 | tf_op jit(solution)/shard_map/psum | solution.py:124
  477.2 6.4 fusion.1
  483.6 1.3 slice_bitcast_fusion
  486.8 0.8 copy-done.11
  487.6 0.6 copy-done.12
  488.2 70.5 %subtract_reduce_fusion.2 = (bf16[32,16,1024]{2,1,0:T(8,128)(2,1)S(1)}, bf16[32,16,1024]{2,1,0:T(8,128)(2,1)S(1)}, f32[32,16,1024]{2,1,0:T(8,128)S(1)}, f32[32,1...) fusion(f32[16,16,1024]{2,1,0:T(8,128)S(1)} %get-tuple-element.5, ...), kind=kLoop, calls=%fused_computation.5 | loop fusion | flops 264241152 | bytes 23068672 | tf_op jit(solution)/shard_map/reduce_sum | solution.py:80
  558.7 1.9 pad_maximum_fusion.5
  560.6 6.5 collective-permute-start.5
  567.3 3.0 collective-permute-start.4
  570.3 1.5 pad_maximum_fusion.3
  571.7 1.9 collective-permute-start.3
  573.7 20.6 %add_reduce_fusion.4 = (f32[32,16,1024]{2,1,0:T(8,128)S(1)}, f32[32,16,1024]{2,1,0:T(8,128)S(1)}) fusion(f32[16,16,1024]{2,1,0:T(8,128)S(1)} %get-tuple-element.60, f32[16,16,1024]{2,1,0:T(8,128)S(1)} %get-tuple-element.59, f32[32,16,1024]{2,1,0:T(8,128)S(1)} %copy-done.9, f32[32,16,1024]{2,1,0:T(8,128)S(1)} %copy-done.10), kind=kLoop, calls=%fused_computation.9 | loop fusion | flops 66060288 | bytes 10485760 | tf_op jit(solution)/shard_map/reduce_sum | solution.py:68
  594.3 20.6 %add_reduce_fusion.5 = (f32[32,16,1024]{2,1,0:T(8,128)S(1)}, f32[32,16,1024]{2,1,0:T(8,128)S(1)}) fusion(f32[16,16,1024]{2,1,0:T(8,128)S(1)} %get-tuple-element.62, f32[16,16,1024]{2,1,0:T(8,128)S(1)} %get-tuple-element.61, f32[32,16,1024]{2,1,0:T(8,128)S(1)} %copy-done.8, f32[32,16,1024]{2,1,0:T(8,128)S(1)} %copy-done.7), kind=kLoop, calls=%fused_computation.11 | loop fusion | flops 66060288 | bytes 10485760 | tf_op jit(solution)/shard_map/reduce_sum | solution.py:68
  615.2 1.3 copy-done.4
  616.5 20.5 %add_reduce_fusion.6 = (f32[32,16,1024]{2,1,0:T(8,128)S(1)}, f32[32,16,1024]{2,1,0:T(8,128)S(1)}) fusion(f32[16,16,1024]{2,1,0:T(8,128)S(1)} %get-tuple-element.64, f32[16,16,1024]{2,1,0:T(8,128)S(1)} %get-tuple-element.63, f32[32,16,1024]{2,1,0:T(8,128)S(1)} %copy-done.4, f32[32,16,1024]{2,1,0:T(8,128)S(1)} %get-tuple-element.49), kind=kLoop, calls=%fused_computation.13 | loop fusion | flops 66060288 | bytes 10485760 | tf_op jit(solution)/shard_map/reduce_sum | solution.py:68
  637.1 17.6 %collective-permute-done.4 = bf16[32,16,2048]{2,1,0:T(8,128)(2,1)} collective-permute-done((bf16[32,16,2048]{2,1,0:T(8,128)(2,1)S(1)}, bf16[32,16,2048]{2,1,0:T(8,128)(2,1)}, u32[]{:S(2)}, u32[]{:S(2)}) %collective-permute-start.4) | collective-permute-done | bytes 2097184 | tf_op jit(solution)/shard_map/ppermute | solution.py:16
  654.6 22.6 %collective-permute-done.3 = bf16[32,16,2048]{2,1,0:T(8,128)(2,1)} collective-permute-done((bf16[32,16,2048]{2,1,0:T(8,128)(2,1)}, bf16[32,16,2048]{2,1,0:T(8,128)(2,1)}, u32[]{:S(2)}, u32[]{:S(2)}) %collective-permute-start.3) | collective-permute-done | bytes 2097184 | tf_op jit(solution)/shard_map/ppermute | solution.py:16
  677.2 5.7 fusion.25
  682.9 8.8 %all-to-all-start.1 = ((bf16[32,16,2048]{2,1,0:T(8,128)(2,1)}), bf16[32,16,2048]{2,1,0:T(8,128)(2,1)S(1)}, u32[]{:S(2)}, u32[]{:S(2)}) async-start(bf16[32,16,2048]{2,1,0:T(8,128)(2,1)} %fusion.25), calls=%async_computation.1 | async-start | bytes 4194304 | tf_op jit(solution)/shard_map/all_to_all | solution.py:141
  691.7 2.1 dynamic-slice_bitcast_fusion.3
  693.8 25.7 %all-to-all-done.1 = bf16[32,16,2048]{2,1,0:T(8,128)(2,1)S(1)} async-done(((bf16[32,16,2048]{2,1,0:T(8,128)(2,1)}), bf16[32,16,2048]{2,1,0:T(8,128)(2,1)S(1)}, u32[]{:S(2)}, u32[]{:S(2)}) %all-to-all-start.1) | async-done | bytes 2097184 | tf_op jit(solution)/shard_map/all_to_all | solution.py:141
  719.4 2.5 bitcast_convert_fusion
  721.9 5.5 copy.15
  727.4 3.5 fusion.39
  730.9 0.5 slice_add_fusion
  731.8 2.9 bitcast_multiply_fusion.1
  734.7 0.5 copy-done.2
  735.2 0.7 copy-done.6
  735.9 1.4 fusion.40
  737.3 17.7 %fusion.49 = f32[512,2048]{1,0:T(8,128)S(1)} fusion(s32[512]{0:T(512)S(1)} %add_select_fusion.5, pred[512]{0:T(512)(128)(4,1)S(1)} %fusion.61, bf16[512,2048]{0,1:T(8,128)(2,1)S(1)} %fusion.40), kind=kOutput, calls=%fused_computation.107 | convolution fusion | flops 1091567616 | bytes 4721152 | tf_op jit(solution)/shard_map/dot_general | solution.py:150
  755.0 17.8 %fusion.50 = f32[512,2048]{1,0:T(8,128)S(1)} fusion(s32[512]{0:T(512)S(1)} %add_select_fusion.6, pred[512]{0:T(512)(128)(4,1)S(1)} %fusion.62, bf16[512,2048]{0,1:T(8,128)(2,1)S(1)} %fusion.40), kind=kOutput, calls=%fused_computation.108 | convolution fusion | flops 1091567616 | bytes 4721152 | tf_op jit(solution)/shard_map/dot_general | solution.py:150
  772.8 18.1 %fusion.51 = f32[512,2048]{1,0:T(8,128)S(1)} fusion(s32[512]{0:T(512)S(1)} %add_select_fusion.7, pred[512]{0:T(512)(128)(4,1)S(1)} %iota_compare_fusion, bf16[512,2048]{0,1:T(8,128)(2,1)S(1)} %fusion.40), kind=kOutput, calls=%fused_computation.109 | convolution fusion | flops 1091567616 | bytes 4721152 | tf_op jit(solution)/shard_map/dot_general | solution.py:150
  791.0 19.0 %fusion.38 = bf16[1,512,2048]{2,1,0:T(8,128)(2,1)} fusion(f32[512,2048]{1,0:T(8,128)S(1)} %fusion.49, f32[512,2048]{1,0:T(8,128)S(1)} %fusion.51, f32[512,2048]{1,0:T(8,128)S(1)} %fusion.50, s32[512]{0:T(512)S(1)} %add_select_fusion.4, pred[512]{0:T(512)(128)(4,1)S(1)} %fusion.60, bf16[512,2048]{0,1:T(8,128)(2,1)S(1)} %fusion.40), kind=kOutput, calls=%fused_computation.84 | convolution fusion | flops 1095761920 | bytes 15206912 | tf_op jit(solution)/shard_map/dot_general | solution.py:150
  (74 shorter events, 4.8 us)
Async XLA Ops:
  7.2 1.6 copy-start
  7.2 470.0 %all-reduce.4.cloned.1.call-start = ((), (), s32[]{:S(2)}) async-start(), calls=%async_computation.2 | async-start | bytes 12582912 | tf_op jit(solution)/shard_map/psum | solution.py:124
  43.4 34.8 %copy-start.13 = (f32[512,512]{1,0:T(8,128)}, f32[512,512]{1,0:T(8,128)S(1)}, u32[]{:S(2)}) copy-start(f32[512,512]{1,0:T(8,128)S(1)} %fusion.43) | copy-start | bytes 3145732
  61.0 17.2 %copy-start.15 = (f32[512,512]{1,0:T(8,128)}, f32[512,512]{1,0:T(8,128)S(1)}, u32[]{:S(2)}) copy-start(f32[512,512]{1,0:T(8,128)S(1)} %fusion.45) | copy-start | bytes 3145732
  78.2 1.0 copy-start.17
  79.2 2.0 copy-start.3
  82.6 3.9 copy-start.5
  157.6 8.4 %copy-start.25 = (s32[1,3]{1,0:T(1,128)S(1)}, s32[1,3]{1,0:T(1,128)}, u32[]{:S(2)}) copy-start(s32[1,3]{1,0:T(1,128)} %param.4) | copy-start | bytes 40
  161.1 28.9 %collective-permute-start.2 = (bf16[32,16,2048]{2,1,0:T(8,128)(2,1)S(1)}, bf16[32,16,2048]{2,1,0:T(8,128)(2,1)S(1)}, u32[]{:S(2)}, u32[]{:S(2)}) collective-permute-start(bf16[32,16,2048]{2,1,0:T(8,128)(2,1)S(1)} %bitcast.111), channel_id=1, source_target_pairs={{24,0},{32,8},{40,16},{48,24},{56,32},{64,40},{72,48},{80,56},{88,... | collective-permute-start | bytes 6291464 | tf_op jit(solution)/shard_map/ppermute | solution.py:16
  162.4 91.2 %collective-permute-start.1 = (bf16[32,16,2048]{2,1,0:T(8,128)(2,1)S(1)}, bf16[32,16,2048]{2,1,0:T(8,128)(2,1)S(1)}, u32[]{:S(2)}, u32[]{:S(2)}) collective-permute-start(bf16[32,16,2048]{2,1,0:T(8,128)(2,1)S(1)} %bitcast.112), channel_id=1, source_target_pairs={{16,0},{24,8},{32,16},{40,24},{48,32},{56,40},{64,48},{72,56},{80,... | collective-permute-start | bytes 6291464 | tf_op jit(solution)/shard_map/ppermute | solution.py:16
  163.7 91.9 %collective-permute-start = (bf16[32,16,2048]{2,1,0:T(8,128)(2,1)S(1)}, bf16[32,16,2048]{2,1,0:T(8,128)(2,1)S(1)}, u32[]{:S(2)}, u32[]{:S(2)}) collective-permute-start(bf16[32,16,2048]{2,1,0:T(8,128)(2,1)S(1)} %bitcast.113), channel_id=1, source_target_pairs={{8,0},{16,8},{24,16},{32,24},{40,32},{48,40},{56,48},{64,56},{72,6... | collective-permute-start | bytes 6291464 | tf_op jit(solution)/shard_map/ppermute | solution.py:16
  299.1 1.9 copy-start.23
  299.1 2.2 copy-start.24
  299.1 2.5 copy-start.21
  299.1 2.8 copy-start.22
  486.0 1.6 copy-start.11
  486.0 2.2 copy-start.12
  558.7 8.4 %copy-start.19 = (bf16[32,16,1024]{2,1,0:T(8,128)(2,1)S(1)}, bf16[32,16,1024]{2,1,0:T(8,128)(2,1)}, u32[]{:S(2)}) copy-start(bf16[32,16,1024]{2,1,0:T(8,128)(2,1)} %get-tuple-element.24) | copy-start | bytes 3145732
  558.7 8.4 %copy-start.20 = (bf16[32,16,1024]{2,1,0:T(8,128)(2,1)S(1)}, bf16[32,16,1024]{2,1,0:T(8,128)(2,1)}, u32[]{:S(2)}) copy-start(bf16[32,16,1024]{2,1,0:T(8,128)(2,1)} %get-tuple-element.25) | copy-start | bytes 3145732
  560.6 76.5 %collective-permute-start.5 = (bf16[32,16,2048]{2,1,0:T(8,128)(2,1)S(1)}, bf16[32,16,2048]{2,1,0:T(8,128)(2,1)}, u32[]{:S(2)}, u32[]{:S(2)}) collective-permute-start(bf16[32,16,2048]{2,1,0:T(8,128)(2,1)S(1)} %pad_maximum_fusion.5), channel_id=1, source_target_pairs={{0,24},{8,32},{16,40},{24,48},{32,56},{40,64},{48,72},{56,80},{64,... | collective-permute-start | bytes 6291464 | tf_op jit(solution)/shard_map/ppermute | solution.py:16
  567.1 6.6 copy-start.9
  567.1 6.6 copy-start.10
  567.3 87.3 %collective-permute-start.4 = (bf16[32,16,2048]{2,1,0:T(8,128)(2,1)S(1)}, bf16[32,16,2048]{2,1,0:T(8,128)(2,1)}, u32[]{:S(2)}, u32[]{:S(2)}) collective-permute-start(bf16[32,16,2048]{2,1,0:T(8,128)(2,1)S(1)} %pad_maximum_fusion.4), channel_id=1, source_target_pairs={{0,16},{8,24},{16,32},{24,40},{32,48},{40,56},{48,64},{56,72},{64,... | collective-permute-start | bytes 6291464 | tf_op jit(solution)/shard_map/ppermute | solution.py:16
  571.7 105.5 %collective-permute-start.3 = (bf16[32,16,2048]{2,1,0:T(8,128)(2,1)}, bf16[32,16,2048]{2,1,0:T(8,128)(2,1)}, u32[]{:S(2)}, u32[]{:S(2)}) collective-permute-start(bf16[32,16,2048]{2,1,0:T(8,128)(2,1)} %pad_maximum_fusion.3), channel_id=1, source_target_pairs={{0,8},{8,16},{16,24},{24,32},{32,40},{40,48},{48,56},{56,64},{64,7... | collective-permute-start | bytes 6291464 | tf_op jit(solution)/shard_map/ppermute | solution.py:16
  573.7 20.6 %copy-start.7 = (f32[32,16,1024]{2,1,0:T(8,128)S(1)}, f32[32,16,1024]{2,1,0:T(8,128)}, u32[]{:S(2)}) copy-start(f32[32,16,1024]{2,1,0:T(8,128)} %get-tuple-element.68) | copy-start | bytes 6291460
  573.7 20.6 %copy-start.8 = (f32[32,16,1024]{2,1,0:T(8,128)S(1)}, f32[32,16,1024]{2,1,0:T(8,128)}, u32[]{:S(2)}) copy-start(f32[32,16,1024]{2,1,0:T(8,128)} %get-tuple-element.69) | copy-start | bytes 6291460
  594.3 20.6 %copy-start.18 = (bf16[16,16,2048]{2,1,0:T(8,128)(2,1)S(1)}, bf16[16,16,2048]{2,1,0:T(8,128)(2,1)}, u32[]{:S(2)}) copy-start(bf16[16,16,2048]{2,1,0:T(8,128)(2,1)} %get-tuple-element.42) | copy-start | bytes 3145732
  614.9 1.6 copy-start.4
  682.9 36.5 %all-to-all-start.1 = ((bf16[32,16,2048]{2,1,0:T(8,128)(2,1)}), bf16[32,16,2048]{2,1,0:T(8,128)(2,1)S(1)}, u32[]{:S(2)}, u32[]{:S(2)}) async-start(bf16[32,16,2048]{2,1,0:T(8,128)(2,1)} %fusion.25), calls=%async_computation.1 | async-start | bytes 4194304 | tf_op jit(solution)/shard_map/all_to_all | solution.py:141
  721.9 5.5 copy-start.14
  721.9 5.5 copy-start.16
  731.7 3.5 copy-start.2
  731.8 4.1 copy-start.6
  790.9 19.0 %copy-start.1 = (bf16[1,512,2048]{2,1,0:T(8,128)(2,1)S(1)}, bf16[1,512,2048]{2,1,0:T(8,128)(2,1)}, u32[]{:S(2)}) copy-start(bf16[1,512,2048]{2,1,0:T(8,128)(2,1)} %param.3) | copy-start | bytes 6291460
Sparse Core Ops, SparseCore 0:
  305.7 171.4 all-reduce.3
where the time goes:
time: 826 us; the launch traced here: 817 us
  waiting for transfers between devices  315 us (38%)
  other arithmetic  230 us (28%)
  matrix products  142 us (17%)
  local copies, waits for them, and re-layouts  43.9 us (5%)
  blocking collectives  37 us (4%)
  starting transfers between devices  25.1 us (3%)
  between operations  24.1 us (3%)
    psum x1, waiting for transfers between devices, on_device(): totals = lax.psum(correl, 'grp')  164 us
    ppermute x6, waiting for transfers between devices, passed_along(): return lax.ppermute(array, axis, pairs)  125 us
    dot_general x4, matrix products, on_device(): jnp.dot(flat_grad[:, start_col:start_col + column_step], tables[table_ind...  72.6 us
    reduce_sum x1, other arithmetic, pull_second(): real_part = jnp.sum(left_real * right_real - left_imag * right_imag, axis=1)  70.5 us
    dot_general x4, matrix products, on_device(): jnp.dot(flat_traces, table_part, preferred_element_type=jnp.float32)  69.4 us
    reduce_sum x3, other arithmetic, pull_first(): real_part = jnp.sum(left_real * right_real + left_imag * right_imag, axis=2)  61.7 us
    all_to_all x1, blocking collectives, on_device(): lax.all_to_all(whitened, 'win', split_axis=1, concat_axis=0, tiled=True)  37 us
    reduce_sum x1, other arithmetic, correlate(): real_sum = jnp.sum(left_real * right_real + left_imag * right_imag, axis=0)  35.8 us
  transfers between devices with their start and end apart: 8, of which 7 were waited for; matrix products, arithmetic and copies ran while one was open for 8% of the time, Pallas kernels for 0%

commit v1 on v0

--- a/solution.py
+++ b/solution.py
@@ -121,7 +121,9 @@
         * live_slots
     )
     share_start = lax.axis_index("grp") * share_width
-    totals = lax.psum(correl, "grp")
+    totals = correl
+    for hop in (1, 2, 4):
+        totals = totals + lax.ppermute(totals, "grp", [(dev, dev ^ hop) for dev in range(8)])
     correl_share = lax.dynamic_slice_in_dim(totals, share_start, share_width, 3)
     residual = ((totals - observed[0]) * live_slots).astype(jnp.bfloat16)
     own_grad = pull_first(residual[0], partners[0])

time: 826 us -> 1430 us (1.73)
  waiting for transfers between devices: 315 us -> 653 us
  starting transfers between devices: 25.1 us -> 290 us
    ppermute x0 -> x3, waiting for transfers between devices: none -> 522 us  [on_device(): lax.ppermute(totals, 'grp', [(dev, dev ^ hop) for dev in range(8)])]
    ppermute x0 -> x3, starting transfers between devices: none -> 212 us  [on_device(): lax.ppermute(totals, 'grp', [(dev, dev ^ hop) for dev in range(8)])]
    psum x1 -> x0, waiting for transfers between devices: 164 us -> none  [on_device(): totals = lax.psum(correl, 'grp')]
    ppermute x6, starting transfers between devices: 16.3 us -> 73.4 us  [passed_along(): return lax.ppermute(array, axis, pairs)]
    ppermute x6, waiting for transfers between devices: 125 us -> 106 us  [passed_along(): return lax.ppermute(array, axis, pairs)]
  transfers between devices with their start and end apart: 8 -> 10, of which waited for: 7 -> 8; matrix products, arithmetic and copies ran while one was open for 8% -> 5% of each run, Pallas kernels for 0% -> 0%
where the time goes in v1:
time: 1430 us; the launch traced here: 1420 us
  waiting for transfers between devices  653 us (46%)
  starting transfers between devices  290 us (20%)
  other arithmetic  243 us (17%)
  matrix products  142 us (10%)
  local copies, waits for them, and re-layouts  41.7 us (3%)
  blocking collectives  37 us (3%)
    ppermute x3, waiting for transfers between devices, on_device(): lax.ppermute(totals, 'grp', [(dev, dev ^ hop) for dev in range(8)])  522 us
    ppermute x3, starting transfers between devices, on_device(): lax.ppermute(totals, 'grp', [(dev, dev ^ hop) for dev in range(8)])  212 us
    ppermute x6, waiting for transfers between devices, passed_along(): return lax.ppermute(array, axis, pairs)  106 us
    ppermute x6, starting transfers between devices, passed_along(): return lax.ppermute(array, axis, pairs)  73.4 us
    dot_general x4, matrix products, on_device(): jnp.dot(flat_grad[:, start_col:start_col + column_step], tables[table_ind...  72.6 us
    reduce_sum x1, other arithmetic, pull_second(): real_part = jnp.sum(left_real * right_real - left_imag * right_imag, axis=1)  69.7 us
    dot_general x4, matrix products, on_device(): jnp.dot(flat_traces, table_part, preferred_element_type=jnp.float32)  69.4 us
    reduce_sum x3, other arithmetic, pull_first(): real_part = jnp.sum(left_real * right_real + left_imag * right_imag, axis=2)  61.8 us
  transfers between devices with their start and end apart: 10, of which 8 were waited for; matrix products, arithmetic and copies ran while one was open for 5% of the time, Pallas kernels for 0%

profile of v1, /device:TPU:1, one launch (start us, length us, event | category | flops | bytes accessed | tf_op | source)
XLA Modules:
  0.0 1418.1 jit_solution(4561760752926825286)
XLA Ops:
  0.8 1.5 copy-done
  2.2 17.5 %fusion.41 = f32[512,512]{1,0:T(8,128)S(1)} fusion(bf16[1,512,2048]{2,1,0:T(8,128)(2,1)S(1)} %copy-done, s32[512]{0:T(512)S(1)} %add_select_fusion.4, pred[512]{0:T(512)(128)(4,1)S(1)} %fusion.60), kind=kOutput, calls=%fused_computation.95 | convolution fusion | flops 1091567616 | bytes 3148288 | tf_op jit(solution)/shard_map/dot_general | solution.py:95
  19.7 17.2 %fusion.43 = f32[512,512]{1,0:T(8,128)S(1)} fusion(bf16[1,512,2048]{2,1,0:T(8,128)(2,1)S(1)} %copy-done, s32[512]{0:T(512)S(1)} %add_select_fusion.5, pred[512]{0:T(512)(128)(4,1)S(1)} %fusion.61), kind=kOutput, calls=%fused_computation.97 | convolution fusion | flops 1091567616 | bytes 3148288 | tf_op jit(solution)/shard_map/dot_general | solution.py:95
  36.9 17.6 %fusion.45 = f32[512,512]{1,0:T(8,128)S(1)} fusion(bf16[1,512,2048]{2,1,0:T(8,128)(2,1)S(1)} %copy-done, s32[512]{0:T(512)S(1)} %add_select_fusion.6, pred[512]{0:T(512)(128)(4,1)S(1)} %fusion.62), kind=kOutput, calls=%fused_computation.99 | convolution fusion | flops 1091567616 | bytes 3148288 | tf_op jit(solution)/shard_map/dot_general | solution.py:95
  54.6 17.2 %fusion.47 = f32[512,512]{1,0:T(8,128)S(1)} fusion(bf16[1,512,2048]{2,1,0:T(8,128)(2,1)S(1)} %copy-done, s32[512]{0:T(512)S(1)} %add_select_fusion.7, pred[512]{0:T(512)(128)(4,1)S(1)} %iota_compare_fusion), kind=kOutput, calls=%fused_computation.101 | convolution fusion | flops 1091567616 | bytes 3148288 | tf_op jit(solution)/shard_map/dot_general | solution.py:95
  71.8 2.4 maximum_bitcast_fusion
  74.2 4.4 multiply_add_fusion
  78.6 1.9 reduce_sum.206
  80.8 1.3 copy-done.6
  82.1 2.8 fusion.16
  84.9 10.8 copy.14
  96.3 13.2 reduce.2
  109.4 2.8 reshape.499
  112.2 37.0 %all_to_all.21 = bf16[32,2,16384]{2,1,0:T(2,128)(2,1)S(1)} all-to-all(bf16[32,2,16384]{2,1,0:T(2,128)(2,1)} %reshape.499), channel_id=1, replica_groups=mesh['win'=32,'grp'=8] {'win'}, dimensions={0} | all-to-all | bytes 4194304 | tf_op jit(solution)/shard_map/all_to_all | solution.py:104
  149.2 6.8 reshape.500
  155.9 3.5 copy.17
  159.4 1.3 collective-permute-start.2
  160.7 1.3 collective-permute-start.1
  162.0 2.7 collective-permute-start
  167.4 2.4 slice_convert_fusion.7
  169.8 18.5 %collective-permute-done.2 = bf16[32,16,2048]{2,1,0:T(8,128)(2,1)S(1)} collective-permute-done((bf16[32,16,2048]{2,1,0:T(8,128)(2,1)S(1)}, bf16[32,16,2048]{2,1,0:T(8,128)(2,1)S(1)}, u32[]{:S(2)}, u32[]{:S(2)}) %collective-permute-start.2) | collective-permute-done | bytes 2097184 | tf_op jit(solution)/shard_map/ppermute | solution.py:16
  188.3 63.7 %collective-permute-done.1 = bf16[32,16,2048]{2,1,0:T(8,128)(2,1)S(1)} collective-permute-done((bf16[32,16,2048]{2,1,0:T(8,128)(2,1)S(1)}, bf16[32,16,2048]{2,1,0:T(8,128)(2,1)S(1)}, u32[]{:S(2)}, u32[]{:S(2)}) %collective-permute-start.1) | collective-permute-done | bytes 2097184 | tf_op jit(solution)/shard_map/ppermute | solution.py:16
  252.0 1.9 collective-permute-done
  253.9 1.1 pad_maximum_fusion
  255.0 1.1 dynamic-slice_bitcast_fusion
  256.1 1.8 slice_convert_fusion.6
  257.9 3.9 slice_convert_fusion
  261.8 35.3 %add_reduce_fusion.9 = (f32[16,16,1024]{2,1,0:T(8,128)S(1)}, f32[16,16,1024]{2,1,0:T(8,128)}, f32[16,16,1024]{2,1,0:T(8,128)}, f32[16,16,1024]{2,1,0:T(8,128)}, ...) fusion(f32[32,16,1024]{2,1,0:T(8,128)} %get-tuple-element.52, f32[32,16,1024]{2,1,0:T(8,128)} %get-tuple-element.50, ...), kind=kLoop, calls=%fused_computation.19 | loop fusion | flops 199753728 | bytes 23068672 | tf_op jit(solution)/shard_map/reduce_sum | solution.py:56
  297.1 1.8 maximum_multiply_fusion.3
  299.8 1.1 maximum_multiply_fusion
  301.0 1.7 collective-permute-start.3
  302.7 131.5 %collective-permute-done.3 = f32[3,16,16,2048]{3,2,1,0:T(8,128)S(1)} collective-permute-done((f32[3,16,16,2048]{3,2,1,0:T(8,128)S(1)}, f32[3,16,16,2048]{3,2,1,0:T(8,128)S(1)}, u32[]{:S(2)}, u32[]{:S(2)}) %collective-permute-start.3) | collective-permute-done | bytes 6291488 | tf_op jit(solution)/shard_map/ppermute | solution.py:126
  434.1 1.3 fusion.100
  435.4 2.7 collective-permute-start.4
  438.1 261.3 %collective-permute-done.4 = f32[3,16,16,2048]{3,2,1,0:T(8,128)S(1)} collective-permute-done((f32[3,16,16,2048]{3,2,1,0:T(8,128)S(1)}, f32[3,16,16,2048]{3,2,1,0:T(8,128)S(1)}, u32[]{:S(2)}, u32[]{:S(2)}) %collective-permute-start.4) | collective-permute-done | bytes 6291488 | tf_op jit(solution)/shard_map/ppermute | solution.py:126
  699.4 3.7 fusion.101
  703.1 207.4 %collective-permute-start.5 = (f32[3,16,16,2048]{3,2,1,0:T(8,128)}, f32[3,16,16,2048]{3,2,1,0:T(8,128)}, u32[]{:S(2)}, u32[]{:S(2)}) collective-permute-start(f32[3,16,16,2048]{3,2,1,0:T(8,128)} %fusion.101), channel_id=1, source_target_pairs={{0,4},{1,5},{2,6},{3,7},{4,0},{5,1},{6,2},{7,3},{8,12},{9,13},{10,... | collective-permute-start | bytes 18874376 | tf_op jit(solution)/shard_map/ppermute | solution.py:126
  918.2 129.2 %collective-permute-done.5 = f32[3,16,16,2048]{3,2,1,0:T(8,128)} collective-permute-done((f32[3,16,16,2048]{3,2,1,0:T(8,128)}, f32[3,16,16,2048]{3,2,1,0:T(8,128)}, u32[]{:S(2)}, u32[]{:S(2)}) %collective-permute-start.5) | collective-permute-done | bytes 6291488 | tf_op jit(solution)/shard_map/ppermute | solution.py:126
  1047.5 12.3 fusion.1
  1062.0 1.1 copy-done.12
  1063.7 69.7 %subtract_reduce_fusion.2 = (bf16[32,16,1024]{2,1,0:T(8,128)(2,1)S(1)}, bf16[32,16,1024]{2,1,0:T(8,128)(2,1)S(1)}, f32[32,16,1024]{2,1,0:T(8,128)S(1)}, f32[32,1...) fusion(f32[16,16,1024]{2,1,0:T(8,128)S(1)} %get-tuple-element.6, ...), kind=kLoop, calls=%fused_computation.5 | loop fusion | flops 264241152 | bytes 23068672 | tf_op jit(solution)/shard_map/reduce_sum | solution.py:80
  1133.4 1.4 pad_maximum_fusion.5
  1134.8 2.6 collective-permute-start.8
  1137.7 63.4 %collective-permute-start.7 = (bf16[32,16,2048]{2,1,0:T(8,128)(2,1)S(1)}, bf16[32,16,2048]{2,1,0:T(8,128)(2,1)S(1)}, u32[]{:S(2)}, u32[]{:S(2)}) collective-permute-start(bf16[32,16,2048]{2,1,0:T(8,128)(2,1)S(1)} %pad_maximum_fusion.4), channel_id=1, source_target_pairs={{0,16},{8,24},{16,32},{24,40},{32,48},{40,56},{48,64},{56,72},{64,... | collective-permute-start | bytes 6291464 | tf_op jit(solution)/shard_map/ppermute | solution.py:16
  1201.0 1.5 pad_maximum_fusion.3
  1202.5 2.1 collective-permute-start.6
  1204.7 20.6 %add_reduce_fusion.6 = (f32[32,16,1024]{2,1,0:T(8,128)S(1)}, f32[32,16,1024]{2,1,0:T(8,128)S(1)}) fusion(f32[16,16,1024]{2,1,0:T(8,128)S(1)} %get-tuple-element.66, f32[16,16,1024]{2,1,0:T(8,128)S(1)} %get-tuple-element.65, f32[32,16,1024]{2,1,0:T(8,128)S(1)} %copy-done.5, f32[32,16,1024]{2,1,0:T(8,128)S(1)} %copy-done.4), kind=kLoop, calls=%fused_computation.13 | loop fusion | flops 66060288 | bytes 10485760 | tf_op jit(solution)/shard_map/reduce_sum | solution.py:68
  1225.3 20.6 %add_reduce_fusion.5 = (f32[32,16,1024]{2,1,0:T(8,128)S(1)}, f32[32,16,1024]{2,1,0:T(8,128)S(1)}) fusion(f32[16,16,1024]{2,1,0:T(8,128)S(1)} %get-tuple-element.64, f32[16,16,1024]{2,1,0:T(8,128)S(1)} %get-tuple-element.63, f32[32,16,1024]{2,1,0:T(8,128)S(1)} %copy-done.11, f32[32,16,1024]{2,1,0:T(8,128)S(1)} %copy-done.10), kind=kLoop, calls=%fused_computation.11 | loop fusion | flops 66060288 | bytes 10485760 | tf_op jit(solution)/shard_map/reduce_sum | solution.py:68
  1246.2 1.3 copy-done.8
  1247.5 20.6 %add_reduce_fusion.4 = (f32[32,16,1024]{2,1,0:T(8,128)S(1)}, f32[32,16,1024]{2,1,0:T(8,128)S(1)}) fusion(f32[16,16,1024]{2,1,0:T(8,128)S(1)} %get-tuple-element.62, f32[16,16,1024]{2,1,0:T(8,128)S(1)} %get-tuple-element.61, f32[32,16,1024]{2,1,0:T(8,128)S(1)} %copy-done.8, f32[32,16,1024]{2,1,0:T(8,128)S(1)} %copy-done.9), kind=kLoop, calls=%fused_computation.9 | loop fusion | flops 66060288 | bytes 10485760 | tf_op jit(solution)/shard_map/reduce_sum | solution.py:68
  1268.1 21.4 %collective-permute-done.6 = bf16[32,16,2048]{2,1,0:T(8,128)(2,1)} collective-permute-done((bf16[32,16,2048]{2,1,0:T(8,128)(2,1)}, bf16[32,16,2048]{2,1,0:T(8,128)(2,1)}, u32[]{:S(2)}, u32[]{:S(2)}) %collective-permute-start.6) | collective-permute-done | bytes 2097184 | tf_op jit(solution)/shard_map/ppermute | solution.py:16
  1289.6 5.3 fusion.25
  1294.8 4.3 all-to-all-start.1
  1299.2 2.1 dynamic-slice_bitcast_fusion.3
  1301.2 25.7 %all-to-all-done.1 = bf16[32,16,2048]{2,1,0:T(8,128)(2,1)S(1)} async-done(((bf16[32,16,2048]{2,1,0:T(8,128)(2,1)}), bf16[32,16,2048]{2,1,0:T(8,128)(2,1)S(1)}, u32[]{:S(2)}, u32[]{:S(2)}) %all-to-all-start.1) | async-done | bytes 2097184 | tf_op jit(solution)/shard_map/all_to_all | solution.py:143
  1327.0 2.5 bitcast_convert_fusion
  1329.5 5.5 copy.15
  1335.0 3.5 fusion.39
  1339.3 2.9 bitcast_multiply_fusion.1
  1343.4 1.8 fusion.40
  1345.2 17.7 %fusion.49 = f32[512,2048]{1,0:T(8,128)S(1)} fusion(s32[512]{0:T(512)S(1)} %add_select_fusion.5, pred[512]{0:T(512)(128)(4,1)S(1)} %copy-done.36, bf16[512,2048]{0,1:T(8,128)(2,1)S(1)} %fusion.40), kind=kOutput, calls=%fused_computation.107 | convolution fusion | flops 1091567616 | bytes 4721152 | tf_op jit(solution)/shard_map/dot_general | solution.py:152
  1363.0 17.8 %fusion.51 = f32[512,2048]{1,0:T(8,128)S(1)} fusion(s32[512]{0:T(512)S(1)} %copy-done.30, pred[512]{0:T(512)(128)(4,1)S(1)} %copy-done.38, bf16[512,2048]{0,1:T(8,128)(2,1)S(1)} %fusion.40), kind=kOutput, calls=%fused_computation.109 | convolution fusion | flops 1091567616 | bytes 4721152 | tf_op jit(solution)/shard_map/dot_general | solution.py:152
  1380.8 18.1 %fusion.50 = f32[512,2048]{1,0:T(8,128)S(1)} fusion(s32[512]{0:T(512)S(1)} %add_select_fusion.6, pred[512]{0:T(512)(128)(4,1)S(1)} %copy-done.34, bf16[512,2048]{0,1:T(8,128)(2,1)S(1)} %fusion.40), kind=kOutput, calls=%fused_computation.108 | convolution fusion | flops 1091567616 | bytes 4721152 | tf_op jit(solution)/shard_map/dot_general | solution.py:152
  1399.0 19.0 %fusion.38 = bf16[1,512,2048]{2,1,0:T(8,128)(2,1)} fusion(f32[512,2048]{1,0:T(8,128)S(1)} %fusion.49, f32[512,2048]{1,0:T(8,128)S(1)} %fusion.51, f32[512,2048]{1,0:T(8,128)S(1)} %fusion.50, s32[512]{0:T(512)S(1)} %copy-done.28, pred[512]{0:T(512)(128)(4,1)S(1)} %copy-done.32, bf16[512,2048]{0,1:T(8,128)(2,1)S(1)} %fusion.40), kind=kOutput, calls=%fused_computation.84 | convolution fusion | flops 1095761920 | bytes 15206912 | tf_op jit(solution)/shard_map/dot_general | solution.py:152
  (105 shorter events, 7.5 us)
Async XLA Ops:
  0.6 1.6 copy-start
  0.7 19.0 %copy-start.27 = (s32[512]{0:T(512)}, s32[512]{0:T(512)S(1)}, u32[]{:S(2)}) copy-start(s32[512]{0:T(512)S(1)} %add_select_fusion.4) | copy-start | bytes 6148
  0.7 19.0 %copy-start.31 = (pred[512]{0:T(512)(128)(4,1)}, pred[512]{0:T(512)(128)(4,1)S(1)}, u32[]{:S(2)}) copy-start(pred[512]{0:T(512)(128)(4,1)S(1)} %fusion.60) | copy-start | bytes 1540
  0.7 19.0 %copy-start.35 = (pred[512]{0:T(512)(128)(4,1)}, pred[512]{0:T(512)(128)(4,1)S(1)}, u32[]{:S(2)}) copy-start(pred[512]{0:T(512)(128)(4,1)S(1)} %fusion.61) | copy-start | bytes 1540
  0.7 36.2 %copy-start.33 = (pred[512]{0:T(512)(128)(4,1)}, pred[512]{0:T(512)(128)(4,1)S(1)}, u32[]{:S(2)}) copy-start(pred[512]{0:T(512)(128)(4,1)S(1)} %fusion.62) | copy-start | bytes 1540
  0.8 53.8 %copy-start.29 = (s32[512]{0:T(512)}, s32[512]{0:T(512)S(1)}, u32[]{:S(2)}) copy-start(s32[512]{0:T(512)S(1)} %add_select_fusion.7) | copy-start | bytes 6148
  2.2 52.3 %copy-start.37 = (pred[512]{0:T(512)(128)(4,1)}, pred[512]{0:T(512)(128)(4,1)S(1)}, u32[]{:S(2)}) copy-start(pred[512]{0:T(512)(128)(4,1)S(1)} %iota_compare_fusion) | copy-start | bytes 1540
  19.7 61.0 %copy-start.14 = (f32[512,512]{1,0:T(8,128)}, f32[512,512]{1,0:T(8,128)S(1)}, u32[]{:S(2)}) copy-start(f32[512,512]{1,0:T(8,128)S(1)} %fusion.41) | copy-start | bytes 3145732
  36.9 34.8 %copy-start.16 = (f32[512,512]{1,0:T(8,128)}, f32[512,512]{1,0:T(8,128)S(1)}, u32[]{:S(2)}) copy-start(f32[512,512]{1,0:T(8,128)S(1)} %fusion.43) | copy-start | bytes 3145732
  54.6 17.2 %copy-start.19 = (f32[512,512]{1,0:T(8,128)}, f32[512,512]{1,0:T(8,128)S(1)}, u32[]{:S(2)}) copy-start(f32[512,512]{1,0:T(8,128)S(1)} %fusion.45) | copy-start | bytes 3145732
  71.7 2.4 copy-start.22
  74.2 7.9 copy-start.17
  74.2 7.9 copy-start.20
  80.7 1.3 copy-start.6
  155.9 8.8 copy-start.26
  159.4 28.9 %collective-permute-start.2 = (bf16[32,16,2048]{2,1,0:T(8,128)(2,1)S(1)}, bf16[32,16,2048]{2,1,0:T(8,128)(2,1)S(1)}, u32[]{:S(2)}, u32[]{:S(2)}) collective-permute-start(bf16[32,16,2048]{2,1,0:T(8,128)(2,1)S(1)} %bitcast.111), channel_id=1, source_target_pairs={{24,0},{32,8},{40,16},{48,24},{56,32},{64,40},{72,48},{80,56},{88,... | collective-permute-start | bytes 6291464 | tf_op jit(solution)/shard_map/ppermute | solution.py:16
  160.7 91.2 %collective-permute-start.1 = (bf16[32,16,2048]{2,1,0:T(8,128)(2,1)S(1)}, bf16[32,16,2048]{2,1,0:T(8,128)(2,1)S(1)}, u32[]{:S(2)}, u32[]{:S(2)}) collective-permute-start(bf16[32,16,2048]{2,1,0:T(8,128)(2,1)S(1)} %bitcast.112), channel_id=1, source_target_pairs={{16,0},{24,8},{32,16},{40,24},{48,32},{56,40},{64,48},{72,56},{80,... | collective-permute-start | bytes 6291464 | tf_op jit(solution)/shard_map/ppermute | solution.py:16
  162.0 91.9 %collective-permute-start = (bf16[32,16,2048]{2,1,0:T(8,128)(2,1)S(1)}, bf16[32,16,2048]{2,1,0:T(8,128)(2,1)S(1)}, u32[]{:S(2)}, u32[]{:S(2)}) collective-permute-start(bf16[32,16,2048]{2,1,0:T(8,128)(2,1)S(1)} %bitcast.113), channel_id=1, source_target_pairs={{8,0},{16,8},{24,16},{32,24},{40,32},{48,40},{56,48},{64,56},{72,6... | collective-permute-start | bytes 6291464 | tf_op jit(solution)/shard_map/ppermute | solution.py:16
  257.9 3.9 copy-start.3
  297.1 1.9 copy-start.24
  297.1 2.2 copy-start.25
  297.1 2.5 copy-start.23
  301.0 133.2 %collective-permute-start.3 = (f32[3,16,16,2048]{3,2,1,0:T(8,128)S(1)}, f32[3,16,16,2048]{3,2,1,0:T(8,128)S(1)}, u32[]{:S(2)}, u32[]{:S(2)}) collective-permute-start(f32[3,16,16,2048]{3,2,1,0:T(8,128)S(1)} %maximum_multiply_fusion), channel_id=1, source_target_pairs={{0,1},{1,0},{2,3},{3,2},{4,5},{5,4},{6,7},{7,6},{8,9},{9,8},{10,11... | collective-permute-start | bytes 18874376 | tf_op jit(solution)/shard_map/ppermute | solution.py:126
  435.4 264.0 %collective-permute-start.4 = (f32[3,16,16,2048]{3,2,1,0:T(8,128)S(1)}, f32[3,16,16,2048]{3,2,1,0:T(8,128)S(1)}, u32[]{:S(2)}, u32[]{:S(2)}) collective-permute-start(f32[3,16,16,2048]{3,2,1,0:T(8,128)S(1)} %fusion.100), channel_id=1, source_target_pairs={{0,2},{1,3},{2,0},{3,1},{4,6},{5,7},{6,4},{7,5},{8,10},{9,11},{10,... | collective-permute-start | bytes 18874376 | tf_op jit(solution)/shard_map/ppermute | solution.py:126
  703.1 344.4 %collective-permute-start.5 = (f32[3,16,16,2048]{3,2,1,0:T(8,128)}, f32[3,16,16,2048]{3,2,1,0:T(8,128)}, u32[]{:S(2)}, u32[]{:S(2)}) collective-permute-start(f32[3,16,16,2048]{3,2,1,0:T(8,128)} %fusion.101), channel_id=1, source_target_pairs={{0,4},{1,5},{2,6},{3,7},{4,0},{5,1},{6,2},{7,3},{8,12},{9,13},{10,... | collective-permute-start | bytes 18874376 | tf_op jit(solution)/shard_map/ppermute | solution.py:126
  1061.5 1.6 copy-start.12
  1061.5 2.2 copy-start.13
  1134.8 133.3 %collective-permute-start.8 = (bf16[32,16,2048]{2,1,0:T(8,128)(2,1)S(1)}, bf16[32,16,2048]{2,1,0:T(8,128)(2,1)}, u32[]{:S(2)}, u32[]{:S(2)}) collective-permute-start(bf16[32,16,2048]{2,1,0:T(8,128)(2,1)S(1)} %pad_maximum_fusion.5), channel_id=1, source_target_pairs={{0,24},{8,32},{16,40},{24,48},{32,56},{40,64},{48,72},{56,80},{64,... | collective-permute-start | bytes 6291464 | tf_op jit(solution)/shard_map/ppermute | solution.py:16
  1137.5 67.2 %copy-start.4 = (f32[32,16,1024]{2,1,0:T(8,128)S(1)}, f32[32,16,1024]{2,1,0:T(8,128)}, u32[]{:S(2)}) copy-start(f32[32,16,1024]{2,1,0:T(8,128)} %copy-done.3) | copy-start | bytes 6291460
  1137.5 67.2 %copy-start.5 = (f32[32,16,1024]{2,1,0:T(8,128)S(1)}, f32[32,16,1024]{2,1,0:T(8,128)}, u32[]{:S(2)}) copy-start(f32[32,16,1024]{2,1,0:T(8,128)} %get-tuple-element.52) | copy-start | bytes 6291460
  1137.7 130.4 %collective-permute-start.7 = (bf16[32,16,2048]{2,1,0:T(8,128)(2,1)S(1)}, bf16[32,16,2048]{2,1,0:T(8,128)(2,1)S(1)}, u32[]{:S(2)}, u32[]{:S(2)}) collective-permute-start(bf16[32,16,2048]{2,1,0:T(8,128)(2,1)S(1)} %pad_maximum_fusion.4), channel_id=1, source_target_pairs={{0,16},{8,24},{16,32},{24,40},{32,48},{40,56},{48,64},{56,72},{64,... | collective-permute-start | bytes 6291464 | tf_op jit(solution)/shard_map/ppermute | solution.py:16
  1202.5 87.1 %collective-permute-start.6 = (bf16[32,16,2048]{2,1,0:T(8,128)(2,1)}, bf16[32,16,2048]{2,1,0:T(8,128)(2,1)}, u32[]{:S(2)}, u32[]{:S(2)}) collective-permute-start(bf16[32,16,2048]{2,1,0:T(8,128)(2,1)} %pad_maximum_fusion.3), channel_id=1, source_target_pairs={{0,8},{8,16},{16,24},{24,32},{32,40},{40,48},{48,56},{56,64},{64,7... | collective-permute-start | bytes 6291464 | tf_op jit(solution)/shard_map/ppermute | solution.py:16
  1204.7 20.6 %copy-start.10 = (f32[32,16,1024]{2,1,0:T(8,128)S(1)}, f32[32,16,1024]{2,1,0:T(8,128)}, u32[]{:S(2)}) copy-start(f32[32,16,1024]{2,1,0:T(8,128)} %get-tuple-element.70) | copy-start | bytes 6291460
  1204.7 20.6 %copy-start.11 = (f32[32,16,1024]{2,1,0:T(8,128)S(1)}, f32[32,16,1024]{2,1,0:T(8,128)}, u32[]{:S(2)}) copy-start(f32[32,16,1024]{2,1,0:T(8,128)} %get-tuple-element.71) | copy-start | bytes 6291460
  1225.3 20.9 %copy-start.9 = (f32[32,16,1024]{2,1,0:T(8,128)S(1)}, f32[32,16,1024]{2,1,0:T(8,128)}, u32[]{:S(2)}) copy-start(f32[32,16,1024]{2,1,0:T(8,128)} %get-tuple-element.46) | copy-start | bytes 6291460
  1245.9 1.6 copy-start.8
  1294.8 32.1 %all-to-all-start.1 = ((bf16[32,16,2048]{2,1,0:T(8,128)(2,1)}), bf16[32,16,2048]{2,1,0:T(8,128)(2,1)S(1)}, u32[]{:S(2)}, u32[]{:S(2)}) async-start(bf16[32,16,2048]{2,1,0:T(8,128)(2,1)} %fusion.25), calls=%async_computation.1 | async-start | bytes 4194304 | tf_op jit(solution)/shard_map/all_to_all | solution.py:143
  1329.5 5.5 copy-start.15
  1329.5 5.5 copy-start.18
  1329.5 5.5 copy-start.21
  1339.3 3.5 copy-start.2
  1339.3 4.1 copy-start.7
  1343.4 1.8 copy-start.36
  1345.2 17.8 %copy-start.30 = (s32[512]{0:T(512)S(1)}, s32[512]{0:T(512)}, u32[]{:S(2)}) copy-start(s32[512]{0:T(512)} %copy-done.29) | copy-start | bytes 6148
  1345.2 17.8 %copy-start.38 = (pred[512]{0:T(512)(128)(4,1)S(1)}, pred[512]{0:T(512)(128)(4,1)}, u32[]{:S(2)}) copy-start(pred[512]{0:T(512)(128)(4,1)} %copy-done.37) | copy-start | bytes 1540
  1363.0 17.8 %copy-start.34 = (pred[512]{0:T(512)(128)(4,1)S(1)}, pred[512]{0:T(512)(128)(4,1)}, u32[]{:S(2)}) copy-start(pred[512]{0:T(512)(128)(4,1)} %copy-done.33) | copy-start | bytes 1540
  1380.8 18.2 %copy-start.28 = (s32[512]{0:T(512)S(1)}, s32[512]{0:T(512)}, u32[]{:S(2)}) copy-start(s32[512]{0:T(512)} %copy-done.27) | copy-start | bytes 6148
  1380.8 18.2 %copy-start.32 = (pred[512]{0:T(512)(128)(4,1)S(1)}, pred[512]{0:T(512)(128)(4,1)}, u32[]{:S(2)}) copy-start(pred[512]{0:T(512)(128)(4,1)} %copy-done.31) | copy-start | bytes 1540
  1399.0 19.0 %copy-start.1 = (bf16[1,512,2048]{2,1,0:T(8,128)(2,1)S(1)}, bf16[1,512,2048]{2,1,0:T(8,128)(2,1)}, u32[]{:S(2)}) copy-start(bf16[1,512,2048]{2,1,0:T(8,128)(2,1)} %param.3) | copy-start | bytes 6291460
